TPU v7x, 32 devices: a whole 2x2x4 slice. The times are simulated.
32 devices in a mesh: tm: 4 (over y, x), vox: 8 (over z, core).
Axes of the slice: x: 2, y: 2, z: 4, core: 2. Of those that a mesh axis runs over, the one named last changes fastest.
Arguments:
- u_train: bfloat16 [3072, 4096], P('tm'), may hold values from -0.109375 to 0.109375
- y_train: bfloat16 [3072, 3072], P('tm', 'vox'), may hold values from -6 to 6
- sing: float32 [4096], replicated, may hold values from 0.5 to 8
- lambdas: float32 [20], replicated, may hold values from 0.1 to 100
- lam_index: int32 [24], P('vox'), may hold values from 0 to 19
- live: int32 [24], P('vox'), may hold values from 0 to 1, as said below
- v_basis: bfloat16 [4096, 4096], P('tm', 'vox'), may hold values from -0.09375 to 0.09375
- x_test: bfloat16 [1024, 4096], P(None, 'tm'), may hold values from -0.09375 to 0.09375
Outputs:
- weights: bfloat16 [4096, 3072], P('tm', 'vox')
- predictions: bfloat16 [1024, 3072], P('tm', 'vox')
Inputs may be any that keep to these rules, and one draw needn't show every extreme that they name: Of the 3 voxel blocks that one device along vox holds, at most 2 are live, and some device holds exactly 2.
All inputs are finite; a program needn't handle non-finite values.
Results may differ from a plain program's by a relative error of at most 0.0058.
Values may be sent and summed in bfloat16 or wider, within the bound.
A program may use at most 128 MiB of HBM per device.

v0:
```python
import jax
import jax.numpy as jnp
from jax import lax
from jax.sharding import PartitionSpec as P

BLK = 128


def body(u_train, y_train, sing, lambdas, lam_index, live, v_basis, x_test):
    time_rows = y_train.shape[0]
    column_count = y_train.shape[1]
    block_count = lam_index.shape[0]
    penalty_count = lambdas.shape[0]
    capacity = block_count - block_count // 3
    selector = (lam_index[:, None] == jnp.arange(penalty_count, dtype=jnp.int32)[None, :]).astype(
        jnp.float32
    )
    selector = selector * live[:, None].astype(jnp.float32)
    ranking = jnp.argsort((1 - live) * block_count + jnp.arange(block_count, dtype=jnp.int32))
    picked = ranking[:capacity]
    responses = jnp.take(y_train.reshape(time_rows, block_count, BLK), picked, axis=1)
    responses = responses.reshape(time_rows, capacity * BLK)
    used_selector = jnp.take(selector, picked, axis=0)
    used_columns = responses.shape[1]
    used_blocks = used_selector.shape[0]
    partial_value = lax.dot_general(
        u_train, responses, (((0,), (0,)), ((), ())), preferred_element_type=jnp.float32
    )
    products = lax.psum(partial_value, "tm")
    filters = sing[None, :] / (sing[None, :] * sing[None, :] + lambdas[:, None])
    row_count = products.shape[0]
    blocks = (
        products.reshape(row_count, used_blocks, BLK)
        * jnp.dot(used_selector, filters, precision=lax.Precision.HIGHEST).T[:, :, None]
    )
    filtered = blocks.reshape(row_count, used_columns).astype(jnp.bfloat16)
    weight_sum = jnp.dot(
        lax.all_gather(v_basis, "vox", axis=1, tiled=True),
        filtered,
        preferred_element_type=jnp.float32,
    )
    weight_cols = weight_sum.astype(jnp.bfloat16)
    partial_test = jnp.dot(x_test, weight_cols, preferred_element_type=jnp.float32)
    predicted = lax.psum_scatter(partial_test, "tm", scatter_dimension=0, tiled=True).astype(
        jnp.bfloat16
    )

    def expand(values):
        row_count = values.shape[0]
        placed = jnp.zeros((row_count, block_count, BLK), values.dtype)
        placed = placed.at[:, picked, :].set(values.reshape(row_count, capacity, BLK))
        return placed.reshape(row_count, column_count)

    return (expand(weight_cols), expand(predicted))


def solution(mesh):
    placed = (
        P("tm", None),
        P("tm", "vox"),
        P(),
        P(),
        P("vox"),
        P("vox"),
        P("tm", "vox"),
        P(None, "tm"),
    )
    return jax.shard_map(
        body,
        mesh=mesh,
        in_specs=placed,
        out_specs=(P("tm", "vox"), P("tm", "vox")),
        check_vma=False,
    )
```

profile of v0, /device:TPU:0, one launch (start us, length us, event | category | flops | bytes accessed | tf_op | source)
XLA Modules:
  0.0 177.4 jit_solution(16627243049810682810)
XLA Ops:
  8.0 0.0 copy-start
  8.0 0.0 all-reduce.2.cloned.1.call-start
  8.1 0.8 fusion.10
  8.9 0.7 sort.17
  9.6 1.3 copy.20
  10.9 0.3 copy.21
  11.3 1.3 gather_fusion
  12.6 1.2 copy.22
  13.8 0.1 broadcast_bitcast_fusion
  13.8 0.1 bitcast_select_fusion
  14.0 6.6 %convolution_bitcast_fusion = f32[4096,256]{0,1:T(8,128)} fusion(bf16[768,256]{0,1:T(8,128)(2,1)S(1)} %bitcast_select_fusion, bf16[768,4096]{1,0:T(8,128)(2,1)} %param.8), kind=kOutput, calls=%fused_computation.4 | convolution fusion | flops 1610612736 | bytes 10878976 | tf_op jit(solution)/shard_map/dot_general | solution.py:26
  20.6 0.0 copy-start.2
  20.6 0.0 copy-start.1
  20.6 0.0 copy-start.3
  20.6 0.0 all-reduce.2.cloned.1.call-update
  20.6 0.0 all-gather.2.cloned.1.call-start
  20.7 0.5 all-gather.2.cloned.1.call-update
  21.2 0.0 reduce-scatter.2.cloned.1.call-start
  21.3 0.0 copy-done.2
  21.3 0.1 fusion.5
  21.3 0.6 gather_fusion.1
  21.9 0.0 copy-done.1
  21.9 0.0 copy-done.3
  21.9 0.5 fusion.1
  22.4 104.7 %all-reduce.2.cloned.1.call-done = f32[4096,256]{0,1:T(8,128)} async-done(((f32[4096,256]{0,1:T(8,128)}), f32[4096,256]{0,1:T(8,128)}) %all-reduce.2.cloned.1.call-update) | async-done | bytes 4194320 | tf_op jit(solution)/shard_map/psum | solution.py:29
  127.1 3.9 %fusion = bf16[4096,256]{0,1:T(8,128)(2,1)} fusion(f32[4096,256]{0,1:T(8,128)} %all-reduce.2.cloned.1.call-done, f32[4096,2]{0,1:T(2,128)S(1)} %fusion.1), kind=kLoop, calls=%fused_computation.6 | loop fusion | flops 2097152 | bytes 6324224 | tf_op jit(solution)/shard_map/convert_element_type | solution.py:36
  131.0 0.0 all-gather.2.cloned.1.call-done
  131.0 6.4 %convolution_convert_fusion = bf16[256,1024]{1,0:T(8,128)(2,1)S(1)} fusion(bf16[4096,256]{0,1:T(8,128)(2,1)} %fusion, bf16[1024,4096]{1,0:T(8,128)(2,1)} %all-gather.2.cloned.1.call-done), kind=kOutput, calls=%fused_computation.8 | convolution fusion | flops 2147745792 | bytes 11010048 | tf_op jit(solution)/shard_map/dot_general | solution.py:37
  137.4 0.0 copy-done
  137.4 1.7 convolution_bitcast_fusion.1
  139.1 0.0 reduce-scatter.2.cloned.1.call-update
  139.2 0.3 copy.23
  139.4 0.1 broadcast_in_dim.42
  139.6 0.7 scatter_fusion
  140.3 1.2 copy.24
  141.5 2.3 %copy.27 = bf16[1024,384]{1,0:T(8,128)(2,1)} copy(bf16[1024,384]{0,1:T(8,128)(2,1)} %bitcast.28) | data formatting | bytes 1572864
  143.8 23.4 %reduce-scatter.2.cloned.1.call-done = f32[256,256]{0,1:T(8,128)} async-done(((f32[1024,256]{0,1:T(8,128)}), f32[256,256]{0,1:T(8,128)}) %reduce-scatter.2.cloned.1.call-update) | async-done | bytes 262160 | tf_op jit(solution)/shard_map/reduce_scatter | solution.py:44
  167.3 1.0 convert_element_type.21
  168.2 0.1 copy.25
  168.4 0.6 scatter_fusion.1
  169.0 0.1 copy.26
  169.2 0.8 copy.28
  (5 shorter events, 0.0 us)
Async XLA Ops:
  8.0 129.4 %copy-start = (bf16[1024,1024]{1,0:T(8,128)(2,1)S(1)}, bf16[1024,1024]{1,0:T(8,128)(2,1)}, u32[]{:S(2)}) copy-start(bf16[1024,1024]{1,0:T(8,128)(2,1)} %param.15) | copy-start | bytes 6291460
  8.0 119.1 %all-reduce.2.cloned.1.call-start = ((), (), s32[]{:S(2)}) async-start(), calls=%async_computation.1 | async-start | bytes 8388608 | tf_op jit(solution)/shard_map/psum | solution.py:29
  20.6 0.7 copy-start.2
  20.6 1.3 copy-start.1
  20.6 1.3 copy-start.3
  20.6 110.4 %all-gather.2.cloned.1.call-start = ((), (), s32[]{:S(2)}) async-start(), calls=%async_computation.2 | async-start | bytes 9437184 | tf_op jit(solution)/shard_map/all_gather | solution.py:38
  21.2 146.1 %reduce-scatter.2.cloned.1.call-start = ((), (), s32[]{:S(2)}) async-start(), calls=%async_computation.3 | async-start | bytes 1310720 | tf_op jit(solution)/shard_map/reduce_scatter | solution.py:44
Sparse Core Ops, SparseCore 0:
  20.7 106.3 all-reduce.1
  139.3 27.9 reduce-scatter.1
Sparse Core Ops, SparseCore 1:
  22.7 84.6 all-gather.1
where the time goes:
time: 178 us; the launch traced here: 177 us
  waiting for transfers between devices  129 us (72%)
  between operations  15.6 us (9%)
  matrix products  15.2 us (9%)
  local copies, waits for them, and re-layouts  11.1 us (6%)
  other arithmetic  6.63 us (4%)
    psum x1, waiting for transfers between devices, body(): products = lax.psum(partial_value, 'tm')  105 us
    reduce_scatter x1, waiting for transfers between devices, body(): lax.psum_scatter(partial_test, 'tm', scatter_dimension=0, tiled=True)  23.4 us
    dot_general x1, matrix products, body(): lax.dot_general(u_train, responses, (((0,), (0,)), ((), ())), preferred_e...  6.63 us
    dot_general x1, matrix products, body(): jnp.dot(lax.all_gather(v_basis, 'vox', axis=1, tiled=True), filtered, pre...  6.38 us
    unnamed x11, local copies, waits for them, and re-layouts  4.43 us
    convert_element_type x1, other arithmetic, body(): filtered = blocks.reshape(row_count, used_columns).astype(jnp.bfloat16)  3.9 us
  transfers between devices with their start and end apart: 3, of which 2 were waited for; matrix products, arithmetic and copies ran while one was open for 5% of the time, Pallas kernels for 0%

commit v1 on v0

--- a/solution.py
+++ b/solution.py
@@ -26,7 +26,8 @@
     partial_value = lax.dot_general(
         u_train, responses, (((0,), (0,)), ((), ())), preferred_element_type=jnp.float32
     )
-    products = lax.psum(partial_value, "tm")
+    parts = lax.all_gather(partial_value, "tm")
+    products = jnp.sum(parts, axis=0)
     filters = sing[None, :] / (sing[None, :] * sing[None, :] + lambdas[:, None])
     row_count = products.shape[0]
     blocks = (

time: 178 us -> 309 us (1.74)
  waiting for transfers between devices: 129 us -> 225 us
  local copies, waits for them, and re-layouts: 11.1 us -> 31.9 us
  other arithmetic: 6.63 us -> 21.7 us
    all_gather x0 -> x1, waiting for transfers between devices: none -> 158 us  [body(): parts = lax.all_gather(partial_value, 'tm')]
    psum x1 -> x0, waiting for transfers between devices: 105 us -> none  [body(): products = lax.psum(partial_value, 'tm')]
    all_gather x1, waiting for transfers between devices: 0.01 us -> 44 us  [body(): lax.all_gather(v_basis, 'vox', axis=1, tiled=True)]
    all_gather x0 -> x1, local copies, waits for them, and re-layouts: none -> 20.7 us  [body(): parts = lax.all_gather(partial_value, 'tm')]
    reduce_sum x0 -> x1, other arithmetic: none -> 15.1 us  [body(): products = jnp.sum(parts, axis=0)]
  transfers between devices with their start and end apart: 3 -> 3, of which waited for: 2 -> 3; matrix products, arithmetic and copies ran while one was open for 5% -> 15% of each run, Pallas kernels for 0% -> 0%
where the time goes in v1:
time: 309 us; the launch traced here: 308 us
  waiting for transfers between devices  225 us (73%)
  local copies, waits for them, and re-layouts  31.9 us (10%)
  other arithmetic  21.7 us (7%)
  matrix products  15.2 us (5%)
  between operations  13.9 us (4%)
    all_gather x1, waiting for transfers between devices, body(): parts = lax.all_gather(partial_value, 'tm')  158 us
    all_gather x1, waiting for transfers between devices, body(): lax.all_gather(v_basis, 'vox', axis=1, tiled=True)  44 us
    reduce_scatter x1, waiting for transfers between devices, body(): lax.psum_scatter(partial_test, 'tm', scatter_dimension=0, tiled=True)  21.9 us
    all_gather x1, local copies, waits for them, and re-layouts, body(): parts = lax.all_gather(partial_value, 'tm')  20.7 us
    reduce_sum x1, other arithmetic, body(): products = jnp.sum(parts, axis=0)  15.1 us
    dot_general x1, matrix products, body(): lax.dot_general(u_train, responses, (((0,), (0,)), ((), ())), preferred_e...  6.6 us
    dot_general x1, matrix products, body(): jnp.dot(lax.all_gather(v_basis, 'vox', axis=1, tiled=True), filtered, pre...  6.38 us
  transfers between devices with their start and end apart: 3, of which 3 were waited for; matrix products, arithmetic and copies ran while one was open for 15% of the time, Pallas kernels for 0%

profile of v1, /device:TPU:0, one launch (start us, length us, event | category | flops | bytes accessed | tf_op | source)
XLA Modules:
  0.0 307.6 jit_solution(15315573392722801119)
XLA Ops:
  7.2 0.0 copy-start
  7.2 0.0 all-gather.6.cloned.1.call-start
  7.2 0.8 fusion.10
  8.0 0.7 sort.17
  8.8 1.3 copy.32
  10.1 0.3 copy.33
  10.4 1.3 gather_fusion
  11.8 1.2 copy.34
  12.9 0.1 broadcast_bitcast_fusion
  13.0 0.1 bitcast_select_fusion
  13.1 6.6 %convolution_bitcast_fusion = f32[4096,256]{0,1:T(8,128)} fusion(bf16[768,256]{0,1:T(8,128)(2,1)S(1)} %bitcast_select_fusion, bf16[768,4096]{1,0:T(8,128)(2,1)} %param.8), kind=kOutput, calls=%fused_computation.4 | convolution fusion | flops 1610612736 | bytes 10878976 | tf_op jit(solution)/shard_map/dot_general | solution.py:26
  19.7 0.0 copy-start.2
  19.7 0.0 copy-start.1
  19.7 0.0 copy-start.3
  19.7 0.0 all-gather.6.cloned.1.call-update
  19.8 0.0 all-gather.4.cloned.1.call-start
  19.8 0.7 all-gather.4.cloned.1.call-update
  20.5 0.0 reduce-scatter.2.cloned.1.call-start
  20.6 0.0 copy-done.2
  20.6 0.1 fusion.5
  20.6 0.6 gather_fusion.1
  21.2 0.0 copy-done.1
  21.2 0.0 copy-done.3
  21.2 0.5 fusion.1
  21.7 158.2 %all-gather.6.cloned.1.call-done = f32[16384,256]{0,1:T(8,128)} async-done(((f32[4096,256]{0,1:T(8,128)}), f32[16384,256]{0,1:T(8,128)}) %all-gather.6.cloned.1.call-update) | async-done | bytes 16777232 | tf_op jit(solution)/shard_map/all_gather | solution.py:29
  179.9 20.7 %reshape.75 = f32[4,4096,256]{1,0,2:T(4,128)} reshape(f32[16384,256]{0,1:T(8,128)} %all-gather.6.cloned.1.call-done) | data formatting | bytes 33554432 | tf_op jit(solution)/shard_map/all_gather | solution.py:29
  200.7 15.1 %reduce_sum.9 = f32[4096,256]{0,1:T(8,128)} reduce(f32[4,4096,256]{1,0,2:T(4,128)} %reshape.75, f32[]{:T(128)} %constant.38.clone.1), dimensions={0}, to_apply=%region_1.2 | reduce | flops 3145728 | bytes 20971524 | tf_op jit(solution)/shard_map/reduce_sum | solution.py:30
  215.7 3.9 %fusion = bf16[4096,256]{0,1:T(8,128)(2,1)} fusion(f32[4096,256]{0,1:T(8,128)} %reduce_sum.9, f32[4096,2]{0,1:T(2,128)S(1)} %fusion.1), kind=kLoop, calls=%fused_computation.6 | loop fusion | flops 2097152 | bytes 6324224 | tf_op jit(solution)/shard_map/convert_element_type | solution.py:37
  219.6 44.0 %all-gather.4.cloned.1.call-done = bf16[1024,4096]{1,0:T(8,128)(2,1)} async-done(((bf16[1024,512]{1,0:T(8,128)(2,1)}), bf16[1024,4096]{1,0:T(8,128)(2,1)}) %all-gather.4.cloned.1.call-update) | async-done | bytes 8388624 | tf_op jit(solution)/shard_map/all_gather | solution.py:39
  263.6 6.4 %convolution_convert_fusion = bf16[256,1024]{1,0:T(8,128)(2,1)S(1)} fusion(bf16[4096,256]{0,1:T(8,128)(2,1)} %fusion, bf16[1024,4096]{1,0:T(8,128)(2,1)} %all-gather.4.cloned.1.call-done), kind=kOutput, calls=%fused_computation.8 | convolution fusion | flops 2147745792 | bytes 11010048 | tf_op jit(solution)/shard_map/dot_general | solution.py:38
  270.0 0.0 copy-done
  270.0 1.7 convolution_bitcast_fusion.1
  271.7 0.0 reduce-scatter.2.cloned.1.call-update
  271.8 0.3 copy.35
  272.0 0.1 broadcast_in_dim.42
  272.1 0.7 scatter_fusion
  272.9 1.2 copy.36
  274.1 2.3 copy.39
  276.4 21.9 %reduce-scatter.2.cloned.1.call-done = f32[256,256]{0,1:T(8,128)} async-done(((f32[1024,256]{0,1:T(8,128)}), f32[256,256]{0,1:T(8,128)}) %reduce-scatter.2.cloned.1.call-update) | async-done | bytes 262160 | tf_op jit(solution)/shard_map/reduce_scatter | solution.py:45
  298.3 1.0 convert_element_type.21
  299.3 0.1 copy.37
  299.5 0.6 scatter_fusion.1
  300.1 0.1 copy.38
  300.2 0.8 copy.40
  (5 shorter events, 0.0 us)
Async XLA Ops:
  7.2 262.8 %copy-start = (bf16[1024,1024]{1,0:T(8,128)(2,1)S(1)}, bf16[1024,1024]{1,0:T(8,128)(2,1)}, u32[]{:S(2)}) copy-start(bf16[1024,1024]{1,0:T(8,128)(2,1)} %param.15) | copy-start | bytes 6291460
  7.2 172.7 %all-gather.6.cloned.1.call-start = ((), (), s32[]{:S(2)}) async-start(), calls=%async_computation.3 | async-start | bytes 20971520 | tf_op jit(solution)/shard_map/all_gather | solution.py:29
  19.7 0.8 copy-start.2
  19.7 1.5 copy-start.1
  19.7 1.5 copy-start.3
  19.8 243.8 %all-gather.4.cloned.1.call-start = ((), (), s32[]{:S(2)}) async-start(), calls=%async_computation.1 | async-start | bytes 9437184 | tf_op jit(solution)/shard_map/all_gather | solution.py:39
  20.5 277.8 %reduce-scatter.2.cloned.1.call-start = ((), (), s32[]{:S(2)}) async-start(), calls=%async_computation.2 | async-start | bytes 1310720 | tf_op jit(solution)/shard_map/reduce_scatter | solution.py:45
Sparse Core Ops, SparseCore 0:
  19.9 160.0 all-gather.5
  181.5 82.0 all-gather.3
  271.9 26.4 reduce-scatter.1
